TPU v7x, 256 devices: a whole 4x4x8 slice. The times are simulated.
256 devices in a mesh: seq: 32 (over x_hi, z, core), tp: 8 (over y, x_lo).
Axes of the slice: x: 4 (x_hi: 2, x_lo: 2; x = x_hi * 2 + x_lo), y: 4, z: 8, core: 2. Of those that a mesh axis runs over, the one named last changes fastest.
Arguments:
- queries: bfloat16 [8, 4096, 4096], P('tp', 'seq'), may hold values from -9 to 9
- key_rows: bfloat16 [8, 4096, 4096], P('tp', 'seq'), may hold values from -6 to 6
- values: bfloat16 [8, 4096, 4096], P('tp', 'seq'), may hold values from -6 to 6
- upstream: bfloat16 [8, 4096, 4096], P(None, 'seq', 'tp'), may hold values from -6 to 6
- out_weight: bfloat16 [4096, 4096], P(None, 'tp'), may hold values from -0.09375 to 0.09375
- blocks: int32 [64, 4], replicated, may hold values from 0 to 63, as said below
Outputs:
- attended: bfloat16 [8, 4096, 4096], P('tp', 'seq')
- grad_queries: bfloat16 [8, 4096, 4096], P('tp', 'seq')
- grad_keys: bfloat16 [8, 4096, 4096], P('tp', 'seq')
- grad_values: bfloat16 [8, 4096, 4096], P('tp', 'seq')
- grad_weight: float32 [4096, 4096], P('seq', 'tp')
Inputs may be any that keep to these rules, and one draw needn't show every extreme that they name: Row a lists the blocks a - 1, a and a + 1 modulo 64, then one block 2 to 62 blocks after a modulo 64; no row names a block twice.
All inputs are finite; a program needn't handle non-finite values.
Results may differ from a plain program's by a relative error of at most 0.022.
Values may be sent and summed in bfloat16 or wider, within the bound.
A program may use at most 128 MiB of HBM per device.

v0:
```python
import math
import jax
import jax.numpy as jnp
from jax import lax
from jax.sharding import PartitionSpec as P

HD = 128
BLK = 64
NB = 4


def forward_head(query_rows, key_rows, value_rows, blocks):
    block_count = blocks.shape[0]
    factor = 1.0 / math.sqrt(HD)
    query_tiles = query_rows.reshape(block_count, BLK, HD)
    key_set = key_rows.reshape(block_count, BLK, HD)[blocks].reshape(block_count, NB * BLK, HD)
    value_set = value_rows.reshape(block_count, BLK, HD)[blocks].reshape(block_count, NB * BLK, HD)
    scores = (
        jnp.einsum("qid,qjd->qij", query_tiles, key_set, preferred_element_type=jnp.float32)
        * factor
    )
    row_max = jnp.max(scores, axis=-1, keepdims=True)
    shifted = jnp.exp(scores - row_max)
    soft_probs = shifted / jnp.sum(shifted, axis=-1, keepdims=True)
    probs_low = soft_probs.astype(jnp.bfloat16)
    context = jnp.einsum(
        "qij,qjd->qid", probs_low, value_set, preferred_element_type=jnp.float32
    ).astype(jnp.bfloat16)
    return (context, soft_probs, probs_low, key_set, value_set)


def backward_head(query_rows, grad_rows, blocks, saved):
    context, soft_probs, probs_low, key_set, value_set = saved
    block_count = blocks.shape[0]
    factor = 1.0 / math.sqrt(HD)
    query_tiles = query_rows.reshape(block_count, BLK, HD)
    grad_tiles = grad_rows.reshape(block_count, BLK, HD)
    row_delta = jnp.sum(
        grad_tiles.astype(jnp.float32) * context.astype(jnp.float32), axis=-1, keepdims=True
    )
    dprobs = jnp.einsum("qid,qjd->qij", grad_tiles, value_set, preferred_element_type=jnp.float32)
    dscores = (soft_probs * (dprobs - row_delta) * factor).astype(jnp.bfloat16)
    query_grad = jnp.einsum(
        "qij,qjd->qid", dscores, key_set, preferred_element_type=jnp.float32
    ).astype(jnp.bfloat16)
    flat_list = blocks.reshape(-1)
    key_parts = jnp.einsum(
        "qij,qid->qjd", dscores, query_tiles, preferred_element_type=jnp.float32
    ).reshape(block_count * NB, BLK, HD)
    value_parts = jnp.einsum(
        "qij,qid->qjd", probs_low, grad_tiles, preferred_element_type=jnp.float32
    ).reshape(block_count * NB, BLK, HD)
    key_grad = (
        jnp.zeros((block_count, BLK, HD), jnp.float32)
        .at[flat_list]
        .add(key_parts)
        .astype(jnp.bfloat16)
    )
    value_grad = (
        jnp.zeros((block_count, BLK, HD), jnp.float32)
        .at[flat_list]
        .add(value_parts)
        .astype(jnp.bfloat16)
    )
    return (query_grad, key_grad, value_grad)


def on_device(queries, key_rows, values, upstream, out_weight, blocks):
    head_queries, head_keys, head_values = (
        lax.all_to_all(queries, "seq", split_axis=2, concat_axis=1, tiled=True),
        lax.all_to_all(key_rows, "seq", split_axis=2, concat_axis=1, tiled=True),
        lax.all_to_all(values, "seq", split_axis=2, concat_axis=1, tiled=True),
    )
    length = head_queries.shape[1]
    count_heads = head_queries.shape[2] // HD

    def split_heads(array):
        return array.reshape(length, count_heads, HD).transpose(1, 0, 2)

    def join_heads(array):
        return (
            array.reshape(count_heads, length, HD)
            .transpose(1, 0, 2)
            .reshape(1, length, count_heads * HD)
        )

    grad_tokens = lax.psum_scatter(
        jnp.einsum("stc,dc->std", upstream, out_weight, preferred_element_type=jnp.float32).astype(
            jnp.bfloat16
        ),
        "tp",
        scatter_dimension=0,
        tiled=True,
    )
    grad_heads = lax.all_to_all(grad_tokens, "seq", split_axis=2, concat_axis=1, tiled=True)
    stacked = (
        split_heads(head_queries),
        split_heads(head_keys),
        split_heads(head_values),
        split_heads(grad_heads),
    )

    def both_one(packed):
        saved_one = forward_head(packed[0], packed[1], packed[2], blocks)
        return (saved_one[0],) + backward_head(packed[0], packed[3], blocks, saved_one)

    results = lax.map(both_one, stacked)
    attended, query_grad, key_grad, value_grad = (
        lax.all_to_all(join_heads(results[0]), "seq", split_axis=1, concat_axis=2, tiled=True),
        lax.all_to_all(join_heads(results[1]), "seq", split_axis=1, concat_axis=2, tiled=True),
        lax.all_to_all(join_heads(results[2]), "seq", split_axis=1, concat_axis=2, tiled=True),
        lax.all_to_all(join_heads(results[3]), "seq", split_axis=1, concat_axis=2, tiled=True),
    )
    every_sequence = lax.all_gather(attended, "tp", axis=0, tiled=True)
    grad_weight = lax.psum_scatter(
        jnp.einsum(
            "str,stc->rc", every_sequence, upstream, preferred_element_type=jnp.float32
        ).astype(jnp.bfloat16),
        "seq",
        scatter_dimension=0,
        tiled=True,
    ).astype(jnp.float32)
    return (attended, query_grad, key_grad, value_grad, grad_weight)


def solution(mesh):
    in_specs = (
        P("tp", "seq", None),
        P("tp", "seq", None),
        P("tp", "seq", None),
        P(None, "seq", "tp"),
        P(None, "tp"),
        P(),
    )
    out_specs = (
        P("tp", "seq", None),
        P("tp", "seq", None),
        P("tp", "seq", None),
        P("tp", "seq", None),
        P("seq", "tp"),
    )
    return jax.shard_map(
        on_device, mesh=mesh, in_specs=in_specs, out_specs=out_specs, check_vma=False
    )
```

profile of v0, /device:TPU:32, one launch (start us, length us, event | category | flops | bytes accessed | tf_op | source)
XLA Modules:
  0.0 871.2 jit_solution(8195947875667358401)
XLA Ops:
  8.4 8.9 %convolution_convert_fusion = bf16[8,128,4096]{2,1,0:T(8,128)(2,1)} fusion(bf16[8,128,512]{2,1,0:T(8,128)(2,1)S(1)} %copy-done, bf16[4096,512]{1,0:T(8,128)(2,1)} %param.10), kind=kOutput, calls=%fused_computation.6 | convolution fusion | flops 4299161600 | bytes 13631488 | tf_op jit(solution)/shard_map/stc,dc->std/dot_general | solution.py:88
  17.3 5.0 copy.81
  22.9 23.4 %reduce.1 = bf16[4096,128]{1,0:T(8,128)(2,1)} reduce(bf16[4096,1,128]{2,1,0:T(2,128)(2,1)S(1)} %bitcast.130, bf16[]{:T(256)} %broadcast.81), dimensions={1}, to_apply=%bitcast.71.reduce_sub_computation | reduce | bytes 2097154
  48.4 11.9 %all-to-all-start.2 = ((bf16[32,2,8192]{2,1,0:T(2,128)(2,1)}), bf16[32,2,8192]{2,1,0:T(2,128)(2,1)}, u32[]{:S(2)}, u32[]{:S(2)}) async-start(bf16[32,2,8192]{2,1,0:T(2,128)(2,1)} %reshape.139), calls=%async_computation.2 | async-start | bytes 2097152 | tf_op jit(solution)/shard_map/all_to_all | solution.py:72
  60.3 5.0 copy.76
  65.3 23.4 %reduce.2 = bf16[4096,128]{1,0:T(8,128)(2,1)} reduce(bf16[4096,1,128]{2,1,0:T(2,128)(2,1)S(1)} %bitcast.136, bf16[]{:T(256)} %broadcast.81), dimensions={1}, to_apply=%bitcast.73.reduce_sub_computation | reduce | bytes 2097154
  90.8 9.9 %all-to-all-start = ((bf16[32,2,8192]{2,1,0:T(2,128)(2,1)}), bf16[32,2,8192]{2,1,0:T(2,128)(2,1)}, u32[]{:S(2)}, u32[]{:S(2)}) async-start(bf16[32,2,8192]{2,1,0:T(2,128)(2,1)} %reshape.141), calls=%async_computation | async-start | bytes 2097152 | tf_op jit(solution)/shard_map/all_to_all | solution.py:71
  100.7 5.0 copy.79
  105.8 23.4 %reduce.3 = bf16[4096,128]{1,0:T(8,128)(2,1)} reduce(bf16[4096,1,128]{2,1,0:T(2,128)(2,1)S(1)} %bitcast.137, bf16[]{:T(256)} %broadcast.81), dimensions={1}, to_apply=%bitcast.75.reduce_sub_computation | reduce | bytes 2097154
  131.4 10.1 %all-to-all-start.1 = ((bf16[32,2,8192]{2,1,0:T(2,128)(2,1)}), bf16[32,2,8192]{2,1,0:T(2,128)(2,1)}, u32[]{:S(2)}, u32[]{:S(2)}) async-start(bf16[32,2,8192]{2,1,0:T(2,128)(2,1)} %reshape.143), calls=%async_computation.1 | async-start | bytes 2097152 | tf_op jit(solution)/shard_map/all_to_all | solution.py:70
  141.5 84.0 %reduce-scatter.3.cloned.1.call-done = bf16[1,128,4096]{2,1,0:T(8,128)(2,1)} async-done(((bf16[8,128,4096]{2,1,0:T(8,128)(2,1)}), bf16[1,128,4096]{2,1,0:T(8,128)(2,1)}) %reduce-scatter.3.cloned.1.call-update) | async-done | bytes 1048592 | tf_op jit(solution)/shard_map/reduce_scatter | solution.py:87
  225.5 5.0 copy.85
  230.6 23.4 %reduce = bf16[4096,128]{1,0:T(8,128)(2,1)} reduce(bf16[4096,1,128]{2,1,0:T(2,128)(2,1)S(1)} %bitcast.132, bf16[]{:T(256)} %broadcast.81), dimensions={1}, to_apply=%bitcast.79.reduce_sub_computation | reduce | bytes 2097154
  256.1 9.8 %all-to-all-start.4 = ((bf16[32,2,8192]{2,1,0:T(2,128)(2,1)}), bf16[32,2,8192]{2,1,0:T(2,128)(2,1)}, u32[]{:S(2)}, u32[]{:S(2)}) async-start(bf16[32,2,8192]{2,1,0:T(2,128)(2,1)} %reshape.147), calls=%async_computation.5 | async-start | bytes 2097152 | tf_op jit(solution)/shard_map/all_to_all | solution.py:95
  266.2 4.3 reshape.140
  273.2 5.8 reshape.142
  283.3 3.0 gather_fusion.1
  286.3 3.0 gather_fusion
  289.4 4.3 reshape.144
  296.4 3.8 fusion.24
  302.2 2.9 fusion.21
  305.0 5.8 reshape.148
  313.9 12.7 %multiply_reduce_fusion = (f32[64,64]{1,0:T(8,128)S(1)}, bf16[64,64,128]{2,1,0:T(8,128)(2,1)S(1)}) fusion(bf16[64,64,128]{2,1,0:T(8,128)(2,1)} %bitcast.156, bf16[64,256,128]{2,1,0:T(8,128)(2,1)} %bitcast.149, f32[64,64]{1,0:T(8,128)S(1)} %get-tuple-element.65, f32[64,256,64]{1,2,0:T(8,128)} %copy-done.2), kind=kOutput, calls=%fused_computation.14 | convolution fusion | flops 276300032 | bytes 10518528 | tf_op jit(solution)/shard_map/while/body/eval_jaxpr/qij,qjd->qid/dot_general | solution.py:26
  326.6 17.5 %copy.116 = bf16[1,4096,128]{2,0,1:T(2,128)(2,1)} copy(bf16[1,4096,128]{2,1,0:T(8,128)(2,1)S(1)} %bitcast.155) | data formatting | bytes 2097152 | tf_op jit(solution)/shard_map/reshape;transpose;reshape | solution.py:84
  344.0 23.4 %reduce.4 = bf16[4096,128]{1,0:T(8,128)(2,1)S(1)} reduce(bf16[4096,1,128]{2,1,0:T(2,128)(2,1)} %bitcast.133, bf16[]{:T(256)} %broadcast.81), dimensions={1}, to_apply=%bitcast.113.reduce_sub_computation | reduce | bytes 2097154
  368.6 40.3 %all_to_all.132 = bf16[32,2,8192]{2,1,0:T(2,128)(2,1)S(1)} all-to-all(bf16[32,2,8192]{2,1,0:T(2,128)(2,1)} %reshape.145), channel_id=1, replica_groups=mesh['seq'=32,'tp'=8] {'seq'}, dimensions={0} | all-to-all | bytes 2097152 | tf_op jit(solution)/shard_map/all_to_all | solution.py:109
  408.9 3.5 reshape.146
  417.7 7.5 multiply_convert_fusion
  425.2 158.5 %all-gather.2.cloned.1.call-done = bf16[8,128,4096]{2,1,0:T(8,128)(2,1)} async-done(((bf16[1,128,4096]{2,1,0:T(8,128)(2,1)}), bf16[8,128,4096]{2,1,0:T(8,128)(2,1)}) %all-gather.2.cloned.1.call-update) | async-done | bytes 8388624 | tf_op jit(solution)/shard_map/all_gather | solution.py:114
  583.7 9.7 %bitcast_convert_fusion = bf16[4096,512]{1,0:T(8,128)(2,1)} fusion(bf16[8,128,4096]{2,1,0:T(8,128)(2,1)} %all-gather.2.cloned.1.call-done, bf16[8,128,512]{2,1,0:T(8,128)(2,1)S(1)} %copy-done), kind=kOutput, calls=%fused_computation.5 | convolution fusion | flops 4297064448 | bytes 13631488 | tf_op jit(solution)/shard_map/str,stc->rc/dot_general | solution.py:116
  593.5 3.7 convolution_convert_fusion.1
  597.2 17.0 %copy.115 = bf16[1,4096,128]{2,0,1:T(2,128)(2,1)} copy(bf16[1,4096,128]{2,1,0:T(8,128)(2,1)S(1)} %bitcast.138) | data formatting | bytes 2097152 | tf_op jit(solution)/shard_map/reshape;transpose;reshape | solution.py:84
  614.2 23.5 %reduce.5 = bf16[4096,128]{1,0:T(8,128)(2,1)S(1)} reduce(bf16[4096,1,128]{2,1,0:T(2,128)(2,1)} %bitcast.134, bf16[]{:T(256)} %broadcast.81), dimensions={1}, to_apply=%bitcast.112.reduce_sub_computation | reduce | bytes 2097154
  638.8 10.2 %all-to-all-start.5 = ((bf16[32,2,8192]{2,1,0:T(2,128)(2,1)}), bf16[32,2,8192]{2,1,0:T(2,128)(2,1)}, u32[]{:S(2)}, u32[]{:S(2)}) async-start(bf16[32,2,8192]{2,1,0:T(2,128)(2,1)} %reshape.149), calls=%async_computation.6 | async-start | bytes 2097152 | tf_op jit(solution)/shard_map/all_to_all | solution.py:110
  649.2 6.1 fusion.25
  655.5 26.3 %scatter_fusion = f32[64,64,128]{2,1,0:T(8,128)S(1)} fusion(f32[64,64,128]{2,1,0:T(8,128)S(1)} %broadcast.50.clone, s32[256]{0:T(256)S(1)} %bitcast.159, f32[256,64,128]{2,1,0:T(8,128)} %bitcast.116), kind=kCustom, calls=%fused_computation.2 | custom fusion | flops 2097152 | bytes 25166848 | tf_op jit(solution)/shard_map/while/body/eval_jaxpr/scatter-add | solution.py:56
  682.0 16.7 %copy.114 = bf16[1,4096,128]{2,0,1:T(2,128)(2,1)S(1)} copy(bf16[1,4096,128]{2,1,0:T(8,128)(2,1)S(1)} %bitcast.139) | data formatting | bytes 2097152 | tf_op jit(solution)/shard_map/reshape;transpose;reshape | solution.py:84
  698.8 22.4 %reduce.6 = bf16[4096,128]{1,0:T(8,128)(2,1)S(1)} reduce(bf16[4096,1,128]{2,1,0:T(2,128)(2,1)S(1)} %bitcast.135, bf16[]{:T(256)} %broadcast.81), dimensions={1}, to_apply=%bitcast.111.reduce_sub_computation | reduce | bytes 2097154
  722.3 10.3 %all-to-all-start.6 = ((bf16[32,2,8192]{2,1,0:T(2,128)(2,1)}), bf16[32,2,8192]{2,1,0:T(2,128)(2,1)}, u32[]{:S(2)}, u32[]{:S(2)}) async-start(bf16[32,2,8192]{2,1,0:T(2,128)(2,1)} %reshape.151), calls=%async_computation.7 | async-start | bytes 2097152 | tf_op jit(solution)/shard_map/all_to_all | solution.py:111
  732.6 14.2 %fusion.10 = f32[64,256,128]{2,1,0:T(8,128)} fusion(bf16[64,64,128]{2,1,0:T(8,128)(2,1)S(1)} %bitcast.158, f32[64,64]{1,0:T(8,128)S(1)} %get-tuple-element.65, f32[64,256,64]{1,2,0:T(8,128)} %copy-done.2), kind=kOutput, calls=%fused_computation.24 | convolution fusion | flops 273682688 | bytes 13647872 | tf_op jit(solution)/shard_map/while/body/eval_jaxpr/qij,qid->qjd/dot_general | solution.py:50
  747.0 26.2 %scatter_fusion.1 = f32[64,64,128]{2,1,0:T(8,128)S(1)} fusion(f32[64,64,128]{2,1,0:T(8,128)S(1)} %broadcast.50.clone.1, s32[256]{0:T(256)S(1)} %bitcast.160, f32[256,64,128]{2,1,0:T(8,128)} %bitcast.129), kind=kCustom, calls=%fused_computation.3 | custom fusion | flops 2097152 | bytes 25166848 | tf_op jit(solution)/shard_map/while/body/eval_jaxpr/scatter-add | solution.py:62
  773.5 16.7 %copy.113 = bf16[1,4096,128]{2,0,1:T(2,128)(2,1)S(1)} copy(bf16[1,4096,128]{2,1,0:T(8,128)(2,1)S(1)} %bitcast.140) | data formatting | bytes 2097152 | tf_op jit(solution)/shard_map/reshape;transpose;reshape | solution.py:84
  790.2 22.4 %reduce.7 = bf16[4096,128]{1,0:T(8,128)(2,1)S(1)} reduce(bf16[4096,1,128]{2,1,0:T(2,128)(2,1)S(1)} %bitcast.131, bf16[]{:T(256)} %broadcast.81), dimensions={1}, to_apply=%bitcast.110.reduce_sub_computation | reduce | bytes 2097154
  813.7 9.9 %all-to-all-start.7 = ((bf16[32,2,8192]{2,1,0:T(2,128)(2,1)}), bf16[32,2,8192]{2,1,0:T(2,128)(2,1)}, u32[]{:S(2)}, u32[]{:S(2)}) async-start(bf16[32,2,8192]{2,1,0:T(2,128)(2,1)} %reshape.153), calls=%async_computation.8 | async-start | bytes 2097152 | tf_op jit(solution)/shard_map/all_to_all | solution.py:112
  823.6 4.3 reshape.150
  830.0 4.3 reshape.152
  836.5 17.7 %all-to-all-done.7 = bf16[32,2,8192]{2,1,0:T(2,128)(2,1)} async-done(((bf16[32,2,8192]{2,1,0:T(2,128)(2,1)}), bf16[32,2,8192]{2,1,0:T(2,128)(2,1)}, u32[]{:S(2)}, u32[]{:S(2)}) %all-to-all-start.7) | async-done | bytes 1048608 | tf_op jit(solution)/shard_map/all_to_all | solution.py:112
  854.1 4.4 reshape.154
  (64 shorter events, 46.2 us)
Async XLA Ops:
  7.2 1.2 copy-start
  7.2 218.3 %reduce-scatter.3.cloned.1.call-start = ((), (), s32[]{:S(2)}) async-start(), calls=%async_computation.10 | async-start | bytes 9437184 | tf_op jit(solution)/shard_map/reduce_scatter | solution.py:87
  48.4 42.4 %all-to-all-start.2 = ((bf16[32,2,8192]{2,1,0:T(2,128)(2,1)}), bf16[32,2,8192]{2,1,0:T(2,128)(2,1)}, u32[]{:S(2)}, u32[]{:S(2)}) async-start(bf16[32,2,8192]{2,1,0:T(2,128)(2,1)} %reshape.139), calls=%async_computation.2 | async-start | bytes 2097152 | tf_op jit(solution)/shard_map/all_to_all | solution.py:72
  90.8 40.5 %all-to-all-start = ((bf16[32,2,8192]{2,1,0:T(2,128)(2,1)}), bf16[32,2,8192]{2,1,0:T(2,128)(2,1)}, u32[]{:S(2)}, u32[]{:S(2)}) async-start(bf16[32,2,8192]{2,1,0:T(2,128)(2,1)} %reshape.141), calls=%async_computation | async-start | bytes 2097152 | tf_op jit(solution)/shard_map/all_to_all | solution.py:71
  131.4 124.7 %all-to-all-start.1 = ((bf16[32,2,8192]{2,1,0:T(2,128)(2,1)}), bf16[32,2,8192]{2,1,0:T(2,128)(2,1)}, u32[]{:S(2)}, u32[]{:S(2)}) async-start(bf16[32,2,8192]{2,1,0:T(2,128)(2,1)} %reshape.143), calls=%async_computation.1 | async-start | bytes 2097152 | tf_op jit(solution)/shard_map/all_to_all | solution.py:70
  230.5 35.4 %copy-start.4 = (s32[64,4]{0,1:T(4,128)S(1)}, s32[64,4]{0,1:T(4,128)}, u32[]{:S(2)}) copy-start(s32[64,4]{0,1:T(4,128)} %param.11) | copy-start | bytes 3076
  256.1 49.0 %all-to-all-start.4 = ((bf16[32,2,8192]{2,1,0:T(2,128)(2,1)}), bf16[32,2,8192]{2,1,0:T(2,128)(2,1)}, u32[]{:S(2)}, u32[]{:S(2)}) async-start(bf16[32,2,8192]{2,1,0:T(2,128)(2,1)} %reshape.147), calls=%async_computation.5 | async-start | bytes 2097152 | tf_op jit(solution)/shard_map/all_to_all | solution.py:95
  265.9 317.8 %all-gather.2.cloned.1.call-start = ((), (), s32[]{:S(2)}) async-start(), calls=%async_computation.11 | async-start | bytes 9437184 | tf_op jit(solution)/shard_map/all_gather | solution.py:114
  300.2 2.0 copy-start.2
  417.7 444.9 %reduce-scatter.5.cloned.1.call-start = ((), (), s32[]{:S(2)}) async-start(), calls=%async_computation.12 | async-start | bytes 4325376 | tf_op jit(solution)/shard_map/reduce_scatter | solution.py:115
  638.8 83.5 %all-to-all-start.5 = ((bf16[32,2,8192]{2,1,0:T(2,128)(2,1)}), bf16[32,2,8192]{2,1,0:T(2,128)(2,1)}, u32[]{:S(2)}, u32[]{:S(2)}) async-start(bf16[32,2,8192]{2,1,0:T(2,128)(2,1)} %reshape.149), calls=%async_computation.6 | async-start | bytes 2097152 | tf_op jit(solution)/shard_map/all_to_all | solution.py:110
  721.2 11.4 %copy-start.3 = (bf16[1,32,128,128]{3,2,1,0:T(8,128)(2,1)S(1)}, bf16[1,32,128,128]{3,2,1,0:T(8,128)(2,1)}, u32[]{:S(2)}) copy-start(bf16[1,32,128,128]{3,2,1,0:T(8,128)(2,1)} %copy.86) | copy-start | bytes 3145732
  722.3 91.4 %all-to-all-start.6 = ((bf16[32,2,8192]{2,1,0:T(2,128)(2,1)}), bf16[32,2,8192]{2,1,0:T(2,128)(2,1)}, u32[]{:S(2)}, u32[]{:S(2)}) async-start(bf16[32,2,8192]{2,1,0:T(2,128)(2,1)} %reshape.151), calls=%async_computation.7 | async-start | bytes 2097152 | tf_op jit(solution)/shard_map/all_to_all | solution.py:111
  813.7 40.4 %all-to-all-start.7 = ((bf16[32,2,8192]{2,1,0:T(2,128)(2,1)}), bf16[32,2,8192]{2,1,0:T(2,128)(2,1)}, u32[]{:S(2)}, u32[]{:S(2)}) async-start(bf16[32,2,8192]{2,1,0:T(2,128)(2,1)} %reshape.153), calls=%async_computation.8 | async-start | bytes 2097152 | tf_op jit(solution)/shard_map/all_to_all | solution.py:112
  854.1 10.1 %copy-start.1 = (bf16[8,128,512]{2,1,0:T(8,128)(2,1)S(1)}, bf16[8,128,512]{2,1,0:T(8,128)(2,1)}, u32[]{:S(2)}) copy-start(bf16[8,128,512]{2,1,0:T(8,128)(2,1)} %param.9) | copy-start | bytes 3145732
Sparse Core Ops, SparseCore 0:
  17.5 208.0 reduce-scatter.2
  417.8 165.8 all-gather.1
  593.6 137.1 reduce-scatter.4
where the time goes:
time: 881 us; the launch traced here: 871 us
  waiting for transfers between devices  260 us (30%)
  other arithmetic  243 us (28%)
  local copies, waits for them, and re-layouts  175 us (20%)
  starting transfers between devices  72.2 us (8%)
  matrix products  66.5 us (8%)
  blocking collectives  40.3 us (5%)
  between operations  14.6 us (2%)
    unnamed x8, other arithmetic  185 us
    all_gather x1, waiting for transfers between devices, on_device(): every_sequence = lax.all_gather(attended, 'tp', axis=0, tiled=True)  159 us
    unnamed x43, local copies, waits for them, and re-layouts  84.4 us
    reduce_scatter x1, waiting for transfers between devices, on_device(): lax.psum_scatter(jnp.einsum('stc,dc->std', upstream, out_weight, preferre...  84 us
    another operation x4, local copies, waits for them, and re-layouts, join_heads(): return array.reshape(count_heads, length, HD).transpose(1, 0, 2).reshape(...  68 us
    all_to_all x1, blocking collectives, on_device(): lax.all_to_all(join_heads(results[0]), 'seq', split_axis=1, concat_axis=2...  40.3 us
    scatter-add x1, other arithmetic, backward_head(): key_grad = jnp.zeros((block_count, BLK, HD), jnp.float32).at[flat_list].a...  26.3 us
    scatter-add x1, other arithmetic, backward_head(): value_grad = jnp.zeros((block_count, BLK, HD), jnp.float32).at[flat_list]...  26.2 us
  transfers between devices with their start and end apart: 10, of which 4 were waited for; matrix products, arithmetic and copies ran while one was open for 45% of the time, Pallas kernels for 0%

commit v1 on v0

--- a/solution.py
+++ b/solution.py
@@ -111,7 +111,10 @@
         lax.all_to_all(join_heads(results[2]), "seq", split_axis=1, concat_axis=2, tiled=True),
         lax.all_to_all(join_heads(results[3]), "seq", split_axis=1, concat_axis=2, tiled=True),
     )
-    every_sequence = lax.all_gather(attended, "tp", axis=0, tiled=True)
+    devices = lax.axis_size("tp")
+    parts = jnp.stack([attended for _ in range(devices)])
+    parts = lax.all_to_all(parts, "tp", split_axis=0, concat_axis=0)
+    every_sequence = jnp.concatenate(parts, axis=0)
     grad_weight = lax.psum_scatter(
         jnp.einsum(
             "str,stc->rc", every_sequence, upstream, preferred_element_type=jnp.float32

time: 881 us -> 813 us (0.923)
  waiting for transfers between devices: 260 us -> 187 us
    all_gather x1 -> x0, waiting for transfers between devices: 159 us -> none  [on_device(): every_sequence = lax.all_gather(attended, 'tp', axis=0, tiled=True)]
    all_to_all x0 -> x1, waiting for transfers between devices: none -> 86.5 us  [on_device(): parts = lax.all_to_all(parts, 'tp', split_axis=0, concat_axis=0)]
    unnamed x43 -> x47, local copies, waits for them, and re-layouts: 84.4 us -> 85.4 us
  transfers between devices with their start and end apart: 10 -> 10, of which waited for: 4 -> 4; matrix products, arithmetic and copies ran while one was open for 45% -> 49% of each run, Pallas kernels for 0% -> 0%
where the time goes in v1:
time: 813 us; the launch traced here: 803 us
  other arithmetic  244 us (30%)
  waiting for transfers between devices  187 us (23%)
  local copies, waits for them, and re-layouts  180 us (22%)
  starting transfers between devices  71.9 us (9%)
  matrix products  64.8 us (8%)
  blocking collectives  40.3 us (5%)
  between operations  14.9 us (2%)
    unnamed x8, other arithmetic  186 us
    all_to_all x1, waiting for transfers between devices, on_device(): parts = lax.all_to_all(parts, 'tp', split_axis=0, concat_axis=0)  86.5 us
    unnamed x47, local copies, waits for them, and re-layouts  85.4 us
    reduce_scatter x1, waiting for transfers between devices, on_device(): lax.psum_scatter(jnp.einsum('stc,dc->std', upstream, out_weight, preferre...  84 us
    another operation x4, local copies, waits for them, and re-layouts, join_heads(): return array.reshape(count_heads, length, HD).transpose(1, 0, 2).reshape(...  68 us
    all_to_all x1, blocking collectives, on_device(): lax.all_to_all(join_heads(results[0]), 'seq', split_axis=1, concat_axis=2...  40.3 us
    scatter-add x1, other arithmetic, backward_head(): key_grad = jnp.zeros((block_count, BLK, HD), jnp.float32).at[flat_list].a...  26.2 us
    scatter-add x1, other arithmetic, backward_head(): value_grad = jnp.zeros((block_count, BLK, HD), jnp.float32).at[flat_list]...  26.2 us
  transfers between devices with their start and end apart: 10, of which 4 were waited for; matrix products, arithmetic and copies ran while one was open for 49% of the time, Pallas kernels for 0%

profile of v1, /device:TPU:32, one launch (start us, length us, event | category | flops | bytes accessed | tf_op | source)
XLA Modules:
  0.0 802.8 jit_solution(13075344616487689444)
XLA Ops:
  8.4 8.9 %convolution_convert_fusion = bf16[8,128,4096]{2,1,0:T(8,128)(2,1)} fusion(bf16[8,128,512]{2,1,0:T(8,128)(2,1)S(1)} %copy-done, bf16[4096,512]{1,0:T(8,128)(2,1)} %param.10), kind=kOutput, calls=%fused_computation.8 | convolution fusion | flops 4299161600 | bytes 13631488 | tf_op jit(solution)/shard_map/stc,dc->std/dot_general | solution.py:88
  17.3 5.0 copy.80
  22.9 23.4 %reduce.1 = bf16[4096,128]{1,0:T(8,128)(2,1)} reduce(bf16[4096,1,128]{2,1,0:T(2,128)(2,1)S(1)} %bitcast.137, bf16[]{:T(256)} %broadcast.83), dimensions={1}, to_apply=%bitcast.77.reduce_sub_computation | reduce | bytes 2097154
  48.4 11.9 %all-to-all-start.2 = ((bf16[32,2,8192]{2,1,0:T(2,128)(2,1)}), bf16[32,2,8192]{2,1,0:T(2,128)(2,1)}, u32[]{:S(2)}, u32[]{:S(2)}) async-start(bf16[32,2,8192]{2,1,0:T(2,128)(2,1)} %reshape.148), calls=%async_computation.2 | async-start | bytes 2097152 | tf_op jit(solution)/shard_map/all_to_all | solution.py:72
  60.3 5.0 copy.75
  65.3 23.4 %reduce.2 = bf16[4096,128]{1,0:T(8,128)(2,1)} reduce(bf16[4096,1,128]{2,1,0:T(2,128)(2,1)S(1)} %bitcast.143, bf16[]{:T(256)} %broadcast.83), dimensions={1}, to_apply=%bitcast.79.reduce_sub_computation | reduce | bytes 2097154
  90.8 9.9 %all-to-all-start = ((bf16[32,2,8192]{2,1,0:T(2,128)(2,1)}), bf16[32,2,8192]{2,1,0:T(2,128)(2,1)}, u32[]{:S(2)}, u32[]{:S(2)}) async-start(bf16[32,2,8192]{2,1,0:T(2,128)(2,1)} %reshape.150), calls=%async_computation | async-start | bytes 2097152 | tf_op jit(solution)/shard_map/all_to_all | solution.py:71
  100.7 5.0 copy.78
  105.8 23.4 %reduce.3 = bf16[4096,128]{1,0:T(8,128)(2,1)} reduce(bf16[4096,1,128]{2,1,0:T(2,128)(2,1)S(1)} %bitcast.144, bf16[]{:T(256)} %broadcast.83), dimensions={1}, to_apply=%bitcast.81.reduce_sub_computation | reduce | bytes 2097154
  131.4 10.1 %all-to-all-start.1 = ((bf16[32,2,8192]{2,1,0:T(2,128)(2,1)}), bf16[32,2,8192]{2,1,0:T(2,128)(2,1)}, u32[]{:S(2)}, u32[]{:S(2)}) async-start(bf16[32,2,8192]{2,1,0:T(2,128)(2,1)} %reshape.152), calls=%async_computation.1 | async-start | bytes 2097152 | tf_op jit(solution)/shard_map/all_to_all | solution.py:70
  141.5 84.0 %reduce-scatter.3.cloned.1.call-done = bf16[1,128,4096]{2,1,0:T(8,128)(2,1)} async-done(((bf16[8,128,4096]{2,1,0:T(8,128)(2,1)}), bf16[1,128,4096]{2,1,0:T(8,128)(2,1)}) %reduce-scatter.3.cloned.1.call-update) | async-done | bytes 1048592 | tf_op jit(solution)/shard_map/reduce_scatter | solution.py:87
  225.5 5.0 copy.84
  230.6 23.4 %reduce = bf16[4096,128]{1,0:T(8,128)(2,1)} reduce(bf16[4096,1,128]{2,1,0:T(2,128)(2,1)S(1)} %bitcast.139, bf16[]{:T(256)} %broadcast.83), dimensions={1}, to_apply=%bitcast.85.reduce_sub_computation | reduce | bytes 2097154
  256.1 9.8 %all-to-all-start.4 = ((bf16[32,2,8192]{2,1,0:T(2,128)(2,1)}), bf16[32,2,8192]{2,1,0:T(2,128)(2,1)}, u32[]{:S(2)}, u32[]{:S(2)}) async-start(bf16[32,2,8192]{2,1,0:T(2,128)(2,1)} %reshape.156), calls=%async_computation.5 | async-start | bytes 2097152 | tf_op jit(solution)/shard_map/all_to_all | solution.py:95
  266.1 4.3 reshape.149
  273.2 5.8 reshape.151
  283.3 3.1 gather_fusion.1
  289.4 4.3 reshape.153
  296.4 3.8 fusion.28
  305.0 5.8 reshape.157
  313.8 12.7 %multiply_reduce_fusion = (f32[64,64]{1,0:T(8,128)S(1)}, bf16[64,64,128]{2,1,0:T(8,128)(2,1)S(1)}) fusion(bf16[64,64,128]{2,1,0:T(8,128)(2,1)} %bitcast.162, bf16[64,256,128]{2,1,0:T(8,128)(2,1)} %bitcast.156, f32[64,64]{1,0:T(8,128)S(1)} %get-tuple-element.55, f32[64,256,64]{1,2,0:T(8,128)} %copy-done.2), kind=kOutput, calls=%fused_computation.16 | convolution fusion | flops 276300032 | bytes 10518528 | tf_op jit(solution)/shard_map/while/body/eval_jaxpr/qij,qjd->qid/dot_general | solution.py:26
  326.5 17.5 %copy.113 = bf16[1,4096,128]{2,0,1:T(2,128)(2,1)} copy(bf16[1,4096,128]{2,1,0:T(8,128)(2,1)S(1)} %bitcast.161) | data formatting | bytes 2097152 | tf_op jit(solution)/shard_map/reshape;transpose;reshape | solution.py:84
  343.9 23.4 %reduce.4 = bf16[4096,128]{1,0:T(8,128)(2,1)S(1)} reduce(bf16[4096,1,128]{2,1,0:T(2,128)(2,1)} %bitcast.140, bf16[]{:T(256)} %broadcast.83), dimensions={1}, to_apply=%bitcast.118.reduce_sub_computation | reduce | bytes 2097154
  368.5 40.3 %all_to_all.137 = bf16[32,2,8192]{2,1,0:T(2,128)(2,1)S(1)} all-to-all(bf16[32,2,8192]{2,1,0:T(2,128)(2,1)} %reshape.154), channel_id=1, replica_groups=mesh['seq'=32,'tp'=8] {'seq'}, dimensions={0} | all-to-all | bytes 2097152 | tf_op jit(solution)/shard_map/all_to_all | solution.py:109
  408.8 3.5 reshape.155
  416.5 4.3 stack.5
  420.8 5.0 all-to-all-start.8
  425.9 7.4 multiply_convert_fusion
  433.3 86.5 %all-to-all-done.8 = bf16[8,1,128,4096]{2,3,1,0:T(8,128)(2,1)} async-done(((bf16[8,1,128,4096]{2,3,1,0:T(8,128)(2,1)}), bf16[8,1,128,4096]{2,3,1,0:T(8,128)(2,1)}, u32[]{:S(2)}, u32[]{:S(2)}) %all-to-all-start.8) | async-done | bytes 8388640 | tf_op jit(solution)/shard_map/all_to_all | solution.py:116
  519.8 8.2 %bitcast_convert_fusion = bf16[4096,512]{1,0:T(8,128)(2,1)} fusion(bf16[8,128,512]{2,1,0:T(8,128)(2,1)S(1)} %copy-done, bf16[8,1,128,4096]{2,3,1,0:T(8,128)(2,1)} %all-to-all-done.8), kind=kOutput, calls=%fused_computation.5 | convolution fusion | flops 4297064448 | bytes 13631488 | tf_op jit(solution)/shard_map/str,stc->rc/dot_general | solution.py:119
  528.0 3.7 convolution_convert_fusion.1
  531.7 17.0 %copy.112 = bf16[1,4096,128]{2,0,1:T(2,128)(2,1)} copy(bf16[1,4096,128]{2,1,0:T(8,128)(2,1)S(1)} %bitcast.145) | data formatting | bytes 2097152 | tf_op jit(solution)/shard_map/reshape;transpose;reshape | solution.py:84
  548.7 23.5 %reduce.5 = bf16[4096,128]{1,0:T(8,128)(2,1)S(1)} reduce(bf16[4096,1,128]{2,1,0:T(2,128)(2,1)} %bitcast.141, bf16[]{:T(256)} %broadcast.83), dimensions={1}, to_apply=%bitcast.117.reduce_sub_computation | reduce | bytes 2097154
  573.3 4.9 all-to-all-start.5
  578.4 6.1 fusion.29
  584.8 26.2 %scatter_fusion = f32[64,64,128]{2,1,0:T(8,128)S(1)} fusion(f32[64,64,128]{2,1,0:T(8,128)S(1)} %broadcast.52.clone, s32[256]{0:T(256)S(1)} %bitcast.165, f32[256,64,128]{2,1,0:T(8,128)} %bitcast.121), kind=kCustom, calls=%fused_computation.2 | custom fusion | flops 2097152 | bytes 25166848 | tf_op jit(solution)/shard_map/while/body/eval_jaxpr/scatter-add | solution.py:56
  611.2 16.7 %copy.111 = bf16[1,4096,128]{2,0,1:T(2,128)(2,1)S(1)} copy(bf16[1,4096,128]{2,1,0:T(8,128)(2,1)S(1)} %bitcast.146) | data formatting | bytes 2097152 | tf_op jit(solution)/shard_map/reshape;transpose;reshape | solution.py:84
  628.0 22.4 %reduce.6 = bf16[4096,128]{1,0:T(8,128)(2,1)S(1)} reduce(bf16[4096,1,128]{2,1,0:T(2,128)(2,1)S(1)} %bitcast.142, bf16[]{:T(256)} %broadcast.83), dimensions={1}, to_apply=%bitcast.116.reduce_sub_computation | reduce | bytes 2097154
  651.5 10.3 %all-to-all-start.6 = ((bf16[32,2,8192]{2,1,0:T(2,128)(2,1)}), bf16[32,2,8192]{2,1,0:T(2,128)(2,1)}, u32[]{:S(2)}, u32[]{:S(2)}) async-start(bf16[32,2,8192]{2,1,0:T(2,128)(2,1)} %reshape.160), calls=%async_computation.7 | async-start | bytes 2097152 | tf_op jit(solution)/shard_map/all_to_all | solution.py:111
  661.8 14.1 %fusion.14 = f32[64,256,128]{2,1,0:T(8,128)} fusion(bf16[64,64,128]{2,1,0:T(8,128)(2,1)S(1)} %bitcast.164, f32[64,64]{1,0:T(8,128)S(1)} %get-tuple-element.55, f32[64,256,64]{1,2,0:T(8,128)} %copy-done.2), kind=kOutput, calls=%fused_computation.26 | convolution fusion | flops 273682688 | bytes 13647872 | tf_op jit(solution)/shard_map/while/body/eval_jaxpr/qij,qid->qjd/dot_general | solution.py:50
  676.2 26.2 %scatter_fusion.1 = f32[64,64,128]{2,1,0:T(8,128)S(1)} fusion(f32[64,64,128]{2,1,0:T(8,128)S(1)} %broadcast.52.clone.1, s32[256]{0:T(256)S(1)} %bitcast.166, f32[256,64,128]{2,1,0:T(8,128)} %bitcast.136), kind=kCustom, calls=%fused_computation.3 | custom fusion | flops 2097152 | bytes 25166848 | tf_op jit(solution)/shard_map/while/body/eval_jaxpr/scatter-add | solution.py:62
  702.6 16.7 %copy.110 = bf16[1,4096,128]{2,0,1:T(2,128)(2,1)S(1)} copy(bf16[1,4096,128]{2,1,0:T(8,128)(2,1)S(1)} %bitcast.147) | data formatting | bytes 2097152 | tf_op jit(solution)/shard_map/reshape;transpose;reshape | solution.py:84
  719.4 23.5 %reduce.7 = bf16[4096,128]{1,0:T(8,128)(2,1)} reduce(bf16[4096,1,128]{2,1,0:T(2,128)(2,1)S(1)} %bitcast.138, bf16[]{:T(256)} %broadcast.83), dimensions={1}, to_apply=%bitcast.115.reduce_sub_computation | reduce | bytes 2097154
  745.0 9.9 %all-to-all-start.7 = ((bf16[32,2,8192]{2,1,0:T(2,128)(2,1)}), bf16[32,2,8192]{2,1,0:T(2,128)(2,1)}, u32[]{:S(2)}, u32[]{:S(2)}) async-start(bf16[32,2,8192]{2,1,0:T(2,128)(2,1)} %reshape.162), calls=%async_computation.8 | async-start | bytes 2097152 | tf_op jit(solution)/shard_map/all_to_all | solution.py:112
  756.2 4.3 reshape.159
  762.6 4.3 reshape.161
  769.1 16.3 %all-to-all-done.7 = bf16[32,2,8192]{2,1,0:T(2,128)(2,1)} async-done(((bf16[32,2,8192]{2,1,0:T(2,128)(2,1)}), bf16[32,2,8192]{2,1,0:T(2,128)(2,1)}, u32[]{:S(2)}, u32[]{:S(2)}) %all-to-all-start.7) | async-done | bytes 1048608 | tf_op jit(solution)/shard_map/all_to_all | solution.py:112
  785.4 4.4 reshape.163
  (68 shorter events, 53.4 us)
Async XLA Ops:
  7.2 1.2 copy-start
  7.2 218.3 %reduce-scatter.3.cloned.1.call-start = ((), (), s32[]{:S(2)}) async-start(), calls=%async_computation.11 | async-start | bytes 9437184 | tf_op jit(solution)/shard_map/reduce_scatter | solution.py:87
  48.4 42.4 %all-to-all-start.2 = ((bf16[32,2,8192]{2,1,0:T(2,128)(2,1)}), bf16[32,2,8192]{2,1,0:T(2,128)(2,1)}, u32[]{:S(2)}, u32[]{:S(2)}) async-start(bf16[32,2,8192]{2,1,0:T(2,128)(2,1)} %reshape.148), calls=%async_computation.2 | async-start | bytes 2097152 | tf_op jit(solution)/shard_map/all_to_all | solution.py:72
  90.8 40.5 %all-to-all-start = ((bf16[32,2,8192]{2,1,0:T(2,128)(2,1)}), bf16[32,2,8192]{2,1,0:T(2,128)(2,1)}, u32[]{:S(2)}, u32[]{:S(2)}) async-start(bf16[32,2,8192]{2,1,0:T(2,128)(2,1)} %reshape.150), calls=%async_computation | async-start | bytes 2097152 | tf_op jit(solution)/shard_map/all_to_all | solution.py:71
  131.4 124.7 %all-to-all-start.1 = ((bf16[32,2,8192]{2,1,0:T(2,128)(2,1)}), bf16[32,2,8192]{2,1,0:T(2,128)(2,1)}, u32[]{:S(2)}, u32[]{:S(2)}) async-start(bf16[32,2,8192]{2,1,0:T(2,128)(2,1)} %reshape.152), calls=%async_computation.1 | async-start | bytes 2097152 | tf_op jit(solution)/shard_map/all_to_all | solution.py:70
  230.5 35.3 %copy-start.6 = (s32[64,4]{0,1:T(4,128)S(1)}, s32[64,4]{0,1:T(4,128)}, u32[]{:S(2)}) copy-start(s32[64,4]{0,1:T(4,128)} %param.11) | copy-start | bytes 3076
  256.1 48.9 %all-to-all-start.4 = ((bf16[32,2,8192]{2,1,0:T(2,128)(2,1)}), bf16[32,2,8192]{2,1,0:T(2,128)(2,1)}, u32[]{:S(2)}, u32[]{:S(2)}) async-start(bf16[32,2,8192]{2,1,0:T(2,128)(2,1)} %reshape.156), calls=%async_computation.5 | async-start | bytes 2097152 | tf_op jit(solution)/shard_map/all_to_all | solution.py:95
  300.2 1.9 copy-start.2
  416.5 4.3 copy-start.3
  420.8 98.9 %all-to-all-start.8 = ((bf16[8,1,128,4096]{2,3,1,0:T(8,128)(2,1)}), bf16[8,1,128,4096]{2,3,1,0:T(8,128)(2,1)}, u32[]{:S(2)}, u32[]{:S(2)}) async-start(bf16[8,1,128,4096]{2,3,1,0:T(8,128)(2,1)} %stack.5), calls=%async_computation.9 | async-start | bytes 16777216 | tf_op jit(solution)/shard_map/all_to_all | solution.py:116
  425.8 368.1 %reduce-scatter.5.cloned.1.call-start = ((), (), s32[]{:S(2)}) async-start(), calls=%async_computation.12 | async-start | bytes 4325376 | tf_op jit(solution)/shard_map/reduce_scatter | solution.py:118
  573.3 78.2 %all-to-all-start.5 = ((bf16[32,2,8192]{2,1,0:T(2,128)(2,1)}), bf16[32,2,8192]{2,1,0:T(2,128)(2,1)}, u32[]{:S(2)}, u32[]{:S(2)}) async-start(bf16[32,2,8192]{2,1,0:T(2,128)(2,1)} %reshape.158), calls=%async_computation.6 | async-start | bytes 2097152 | tf_op jit(solution)/shard_map/all_to_all | solution.py:110
  650.4 11.5 %copy-start.5 = (bf16[1,32,128,128]{3,2,1,0:T(8,128)(2,1)S(1)}, bf16[1,32,128,128]{3,2,1,0:T(8,128)(2,1)}, u32[]{:S(2)}) copy-start(bf16[1,32,128,128]{3,2,1,0:T(8,128)(2,1)} %copy.85) | copy-start | bytes 3145732
  651.5 93.5 %all-to-all-start.6 = ((bf16[32,2,8192]{2,1,0:T(2,128)(2,1)}), bf16[32,2,8192]{2,1,0:T(2,128)(2,1)}, u32[]{:S(2)}, u32[]{:S(2)}) async-start(bf16[32,2,8192]{2,1,0:T(2,128)(2,1)} %reshape.160), calls=%async_computation.7 | async-start | bytes 2097152 | tf_op jit(solution)/shard_map/all_to_all | solution.py:111
  719.3 35.5 %copy-start.4 = (bf16[1,128,32,128]{1,3,2,0:T(8,128)(2,1)S(1)}, bf16[1,128,32,128]{1,3,2,0:T(8,128)(2,1)}, u32[]{:S(2)}) copy-start(bf16[1,128,32,128]{1,3,2,0:T(8,128)(2,1)} %copy-done.3) | copy-start | bytes 3145732
  745.0 40.4 %all-to-all-start.7 = ((bf16[32,2,8192]{2,1,0:T(2,128)(2,1)}), bf16[32,2,8192]{2,1,0:T(2,128)(2,1)}, u32[]{:S(2)}, u32[]{:S(2)}) async-start(bf16[32,2,8192]{2,1,0:T(2,128)(2,1)} %reshape.162), calls=%async_computation.8 | async-start | bytes 2097152 | tf_op jit(solution)/shard_map/all_to_all | solution.py:112
  785.4 10.1 %copy-start.1 = (bf16[8,128,512]{2,1,0:T(8,128)(2,1)S(1)}, bf16[8,128,512]{2,1,0:T(8,128)(2,1)}, u32[]{:S(2)}) copy-start(bf16[8,128,512]{2,1,0:T(8,128)(2,1)} %param.9) | copy-start | bytes 3145732
Sparse Core Ops, SparseCore 0:
  17.5 208.0 reduce-scatter.2
  528.1 132.0 reduce-scatter.4
